TPU v7x, 512 devices: a whole 4x4x16 slice. The times are simulated.
512 devices in a mesh: space: 128 (over z, x, core), chan: 4 (over y).
Axes of the slice: x: 4, y: 4, z: 16, core: 2. Of those that a mesh axis runs over, the one named last changes fastest.
Arguments:
- features: bfloat16 [1024, 64, 512], P('space', 'chan'), may hold values from -6 to 6
- weight: bfloat16 [27, 64, 64], P(None, 'chan'), may hold values from -0.15625 to 0.15625
- cotangent: bfloat16 [1024, 64, 512], P('space', 'chan'), may hold values from -6 to 6
- neighbours: int32 [1024, 27], P('space'), may hold values from -1 to 1023, as said below
Outputs:
- output: bfloat16 [1024, 64, 512], P('space', 'chan')
- grad_input: bfloat16 [1024, 64, 512], P('space', 'chan')
- grad_weight: float32 [27, 64, 64], P(None, 'chan')
Inputs may be any that keep to these rules, and one draw needn't show every extreme that they name: `neighbours`: row r lists, for the displacement (i, j, k) in the finite set (-1, 0, 1)^3 at entry 9 (i + 1) + 3 (j + 1) + (k + 1), the slot of the brick at that displacement in bricks, or -1 where the scene has none. Slot s belongs to device s // 8 of space, and a neighbour at first displacement i belongs to the device of index one's own + i. The relation is symmetric: if row r names s at entry m, row s names r at entry 26 - m. A device's occupied bricks fill its first slots, and the last device of space has all 8 slots occupied; an empty slot's row is all -1, no row names an empty slot, and an occupied brick's entry 13 is its own slot.
All inputs are finite; a program needn't handle non-finite values.
Results may differ from a plain program's by a relative error of at most 0.001.
Values may be sent and summed in bfloat16 or wider, within the bound.
A program may use at most 128 MiB of HBM per device.

v0:
```python
import jax
import jax.numpy as jnp
import numpy as np
from jax import lax
from jax.sharding import PartitionSpec as P

flat_width = 896
source_width = 1152


def shifted(shard, axis, by):
    length = lax.axis_size(axis)
    pairs = [(i, i + by) for i in range(length) if 0 <= i + by < length]
    return lax.ppermute(shard, axis, pairs)


def axis_pairs(step):
    if step == 0:
        return [(0, 7)]
    if step == 1:
        return [(place + 1, place) for place in range(8)]
    return [(9, 0)]


def piece_tables():
    lists = []
    positions = []
    for step_x in range(3):
        for step_y in range(3):
            for step_z in range(3):
                source_ids = []
                for grid_x, vox_u in axis_pairs(step_x):
                    for grid_y, vox_v in axis_pairs(step_y):
                        for grid_z, vox_w in axis_pairs(step_z):
                            if step_x == 1:
                                source_ids.append(64 * vox_u + 8 * vox_v + vox_w)
                            else:
                                source_ids.append(8 * vox_v + vox_w)
                            positions.append(100 * grid_x + 10 * grid_y + grid_z)
                lists.append(np.array(source_ids, dtype=np.int32))
    order = np.argsort(np.array(positions, dtype=np.int64)).astype(np.int32)
    return (lists, order)


def grid_tables():
    into_grid = np.zeros((flat_width,), dtype=np.int32)
    valid = np.zeros((flat_width,), dtype=np.float32)
    back_ids = np.zeros((512,), dtype=np.int32)
    for vox_u in range(8):
        for vox_v in range(8):
            for vox_w in range(8):
                place = 100 * vox_u + 10 * vox_v + vox_w
                into_grid[place] = 64 * vox_u + 8 * vox_v + vox_w
                valid[place] = 1.0
                back_ids[64 * vox_u + 8 * vox_v + vox_w] = place
    return (into_grid, valid, back_ids)


def split_planes(bricks):
    return (bricks[..., 0:64], bricks[..., 448:512])


def neighbour_planes(bricks):
    previous = shifted(bricks, "space", 1)
    following = shifted(bricks, "space", -1)
    before_plane = split_planes(previous)[1]
    after_plane = split_planes(following)[0]
    return (before_plane, after_plane)


def spread(own_part):
    entire = lax.all_gather(own_part, "chan", axis=2, tiled=True)
    before_plane, after_plane = neighbour_planes(entire)
    return (entire, before_plane, after_plane)


def assemble(entire, before_plane, after_plane, table, own_start):
    brick_count, depth = (entire.shape[0], entire.shape[1])
    lists, order = piece_tables()
    sources = (
        jnp.concatenate([before_plane, jnp.zeros((1, depth, 64), entire.dtype)], axis=0),
        jnp.concatenate([entire, jnp.zeros((1, depth, 512), entire.dtype)], axis=0),
        jnp.concatenate([after_plane, jnp.zeros((1, depth, 64), entire.dtype)], axis=0),
    )
    pieces = []
    for step_x in range(3):
        block_start = own_start + (step_x - 1) * brick_count
        for step_y in range(3):
            for step_z in range(3):
                index_k = 9 * step_x + 3 * step_y + step_z
                listed = table[:, index_k]
                local_ids = jnp.where(listed < 0, brick_count, listed - block_start)
                picked = jnp.take(sources[step_x], local_ids, axis=0)
                pieces.append(jnp.take(picked, jnp.asarray(lists[index_k]), axis=2))
    joined = jnp.concatenate(pieces, axis=2)
    flat = jnp.take(joined, jnp.asarray(order), axis=2)
    return jnp.pad(flat, ((0, 0), (0, 0), (0, source_width - 1000)))


def to_padded_grid(bricks):
    into_grid, valid, back_ids = grid_tables()
    taken = jnp.take(bricks, jnp.asarray(into_grid), axis=2)
    return taken * jnp.asarray(valid).astype(bricks.dtype)


def from_padded_grid(flat):
    into_grid, valid, back_ids = grid_tables()
    return jnp.take(flat, jnp.asarray(back_ids), axis=2)


def body(features, weight, cotangent, neighbours):
    brick_count, narrow = (features.shape[0], features.shape[1])
    own_start = lax.axis_index("space") * brick_count
    feat_views = tuple((view[0] for view in spread(features[None])))
    grad_views = tuple((view[0] for view in spread(cotangent[None])))
    padded = assemble(feat_views[0], feat_views[1], feat_views[2], neighbours, own_start)
    grad_flat = to_padded_grid(cotangent)
    running = jnp.zeros((brick_count, narrow, flat_width), jnp.float32)
    kernel_terms = []
    for step_x in range(3):
        for step_y in range(3):
            for step_z in range(3):
                index_k = 9 * step_x + 3 * step_y + step_z
                offset = 100 * step_x + 10 * step_y + step_z
                window = padded[:, :, offset : offset + flat_width]
                running = running + jnp.einsum(
                    "oc,rcn->ron", weight[index_k], window, preferred_element_type=jnp.float32
                )
                kernel_terms.append(
                    jnp.einsum("ron,rcn->oc", grad_flat, window, preferred_element_type=jnp.float32)
                )
    output = from_padded_grid(running).astype(jnp.bfloat16)
    voxel_total = brick_count * lax.axis_size("space") * 512
    summed = lax.psum(jnp.stack(kernel_terms), "space")
    grad_weight = summed * voxel_total ** (-0.5)
    full_kernel = lax.all_gather(weight, "chan", axis=1, tiled=True)
    column_start = lax.axis_index("chan") * narrow
    my_kernel = lax.dynamic_slice_in_dim(full_kernel, column_start, narrow, 2)
    grad_padded = assemble(grad_views[0], grad_views[1], grad_views[2], neighbours, own_start)
    backward = jnp.zeros((brick_count, narrow, flat_width), jnp.float32)
    for step_x in range(3):
        for step_y in range(3):
            for step_z in range(3):
                index_k = 9 * step_x + 3 * step_y + step_z
                offset = 100 * step_x + 10 * step_y + step_z
                window = grad_padded[:, :, offset : offset + flat_width]
                backward = backward + jnp.einsum(
                    "oc,ron->rcn",
                    my_kernel[26 - index_k],
                    window,
                    preferred_element_type=jnp.float32,
                )
    grad_input = from_padded_grid(backward).astype(jnp.bfloat16)
    return (output, grad_input, grad_weight)


def solution(mesh):
    in_specs = (
        P("space", "chan", None),
        P(None, "chan", None),
        P("space", "chan", None),
        P("space", None),
    )
    out_specs = (P("space", "chan", None), P("space", "chan", None), P(None, "chan", None))
    return jax.shard_map(body, mesh=mesh, in_specs=in_specs, out_specs=out_specs, check_vma=False)
```

profile of v0, /device:TPU:2, one launch (start us, length us, event | category | flops | bytes accessed | tf_op | source)
XLA Modules:
  0.0 693.8 jit_solution(12567140329959811649)
XLA Ops:
  7.2 15.1 %all-gather = bf16[8,64,512]{2,1,0:T(8,128)(2,1)} all-gather(bf16[8,16,512]{2,1,0:T(8,128)(2,1)} %param.84), channel_id=2, replica_groups=mesh['space'=128,'chan'=4] {'chan'}, dimensions={1}, use_global_device_ids=true | all-gather | bytes 655360 | tf_op jit(solution)/shard_map/all_gather | solution.py:72
  22.4 1.9 collective-permute-start
  24.3 3.6 collective-permute-start.1
  27.9 13.7 %all-gather.1 = bf16[8,64,512]{2,1,0:T(8,128)(2,1)} all-gather(bf16[8,16,512]{2,1,0:T(8,128)(2,1)} %param.86), channel_id=3, replica_groups=mesh['space'=128,'chan'=4] {'chan'}, dimensions={1}, use_global_device_ids=true | all-gather | bytes 655360 | tf_op jit(solution)/shard_map/all_gather | solution.py:72
  41.7 1.9 collective-permute-start.2
  43.6 4.2 collective-permute-start.3
  87.0 1.7 copy.197
  92.9 1.7 copy.199
  96.0 1.7 copy.200
  99.5 1.8 gather_fusion.16
  101.3 1.8 gather_fusion.64
  103.8 2.5 gather_fusion.18
  108.4 1.8 gather_fusion.20
  111.6 2.5 gather_fusion.22
  117.1 2.0 gather_fusion.24
  119.1 2.4 gather_fusion.72
  122.9 1.7 copy.202
  126.3 2.5 gather_fusion.26
  128.8 2.5 gather_fusion.74
  131.5 1.7 copy.203
  136.3 1.7 copy.232
  138.0 1.8 gather_fusion.28
  139.8 1.8 gather_fusion.76
  141.6 1.7 copy.233
  143.3 2.5 gather_fusion.30
  145.9 2.5 gather_fusion.78
  151.7 1.8 gather_fusion.80
  156.0 4.0 gather_fusion
  160.0 4.5 multiply_bitcast_fusion
  164.5 1.7 copy.252
  167.5 14.2 %all_gather.11 = bf16[27,64,64]{2,1,0:T(8,128)(2,1)} all-gather(bf16[27,16,64]{2,1,0:T(8,128)(2,1)S(1)} %copy-done.25), channel_id=1, replica_groups=mesh['space'=128,'chan'=4] {'chan'}, dimensions={1}, use_global_device_ids=true | all-gather | bytes 276480 | tf_op jit(solution)/shard_map/all_gather | solution.py:136
  225.0 1.8 slice_select_fusion.3
  227.5 1.8 slice_select_fusion.2
  229.4 1.8 broadcast_select_fusion.34
  244.0 1.8 broadcast_select_fusion.32
  249.1 2.2 gather_fusion.8
  251.3 2.2 gather_fusion.56
  259.9 1.9 slice_select_fusion.1
  308.1 2.6 bitcast_dynamic-update-slice_fusion
  322.2 5.1 gather_fusion.47
  327.3 2.1 copy.219
  346.1 9.2 %gather_fusion.95 = bf16[1000,8,64]{2,1,0:T(8,128)(2,1)} fusion(bf16[8,64,1000]{1,0,2:T(8,128)(2,1)} %get-tuple-element.60, s32[1024]{0:T(1024)S(1)} %get-tuple-element.187), kind=kCustom, calls=%fused_computation.94.clone | custom fusion | bytes 2052000 | tf_op jit(solution)/shard_map/jit(_take)/gather | solution.py:96
  355.4 2.7 copy.248
  382.6 1.9 copy.250
  384.5 1.8 gather_fusion.96
  387.7 1.9 copy.220
  389.6 1.8 gather_fusion.48
  392.8 292.1 %all-reduce.10.cloned.1.call-done = f32[27,16,64]{2,1,0:T(8,128)} async-done(((f32[27,16,64]{2,1,0:T(8,128)}), f32[27,16,64]{2,1,0:T(8,128)}) %all-reduce.10.cloned.1.call-update) | async-done | bytes 110608 | tf_op jit(solution)/shard_map/psum | solution.py:134
  (510 shorter events, 236.0 us)
Async XLA Ops:
  7.2 46.5 %copy-start = (s32[8,27]{1,0:T(8,128)S(1)}, s32[8,27]{1,0:T(8,128)}, u32[]{:S(2)}) copy-start(s32[8,27]{1,0:T(8,128)} %param.87) | copy-start | bytes 2596
  7.2 677.7 %all-reduce.10.cloned.1.call-start = ((), (), s32[]{:S(2)}) async-start(), calls=%async_computation | async-start | bytes 442368 | tf_op jit(solution)/shard_map/psum | solution.py:134
  22.4 160.4 %collective-permute-start = (bf16[1,8,64,512]{3,2,1,0:T(8,128)(2,1)}, bf16[1,8,64,512]{3,2,1,0:T(8,128)(2,1)}, u32[]{:S(2)}, u32[]{:S(2)}) collective-permute-start(bf16[1,8,64,512]{3,2,1,0:T(8,128)(2,1)} %bitcast), channel_id=1, source_target_pairs={{0,4},{4,8},{8,12},{12,16},{16,20},{20,24},{24,28},{28,32},{32,36}... | collective-permute-start | bytes 1572872 | tf_op jit(solution)/shard_map/ppermute | solution.py:14
  24.3 179.5 %collective-permute-start.1 = (bf16[1,8,64,512]{3,2,1,0:T(8,128)(2,1)}, bf16[1,8,64,512]{3,2,1,0:T(8,128)(2,1)}, u32[]{:S(2)}, u32[]{:S(2)}) collective-permute-start(bf16[1,8,64,512]{3,2,1,0:T(8,128)(2,1)} %bitcast), channel_id=1, source_target_pairs={{4,0},{8,4},{12,8},{16,12},{20,16},{24,20},{28,24},{32,28},{36,32}... | collective-permute-start | bytes 1572872 | tf_op jit(solution)/shard_map/ppermute | solution.py:14
  41.7 140.0 %collective-permute-start.2 = (bf16[1,8,64,512]{3,2,1,0:T(8,128)(2,1)}, bf16[1,8,64,512]{3,2,1,0:T(8,128)(2,1)}, u32[]{:S(2)}, u32[]{:S(2)}) collective-permute-start(bf16[1,8,64,512]{3,2,1,0:T(8,128)(2,1)} %bitcast.89), channel_id=1, source_target_pairs={{0,4},{4,8},{8,12},{12,16},{16,20},{20,24},{24,28},{28,32},{32,36}... | collective-permute-start | bytes 1572872 | tf_op jit(solution)/shard_map/ppermute | solution.py:14
  43.6 161.2 %collective-permute-start.3 = (bf16[1,8,64,512]{3,2,1,0:T(8,128)(2,1)}, bf16[1,8,64,512]{3,2,1,0:T(8,128)(2,1)}, u32[]{:S(2)}, u32[]{:S(2)}) collective-permute-start(bf16[1,8,64,512]{3,2,1,0:T(8,128)(2,1)} %bitcast.89), channel_id=1, source_target_pairs={{4,0},{8,4},{12,8},{16,12},{20,16},{24,20},{28,24},{32,28},{36,32}... | collective-permute-start | bytes 1572872 | tf_op jit(solution)/shard_map/ppermute | solution.py:14
  50.4 35.4 %copy-start.41 = (s32[8]{0:T(128)}, s32[8]{0:T(128)S(1)}, u32[]{:S(2)}) copy-start(s32[8]{0:T(128)S(1)} %get-tuple-element.53) | copy-start | bytes 100
  54.1 99.3 %copy-start.59 = (s32[8]{0:T(128)}, s32[8]{0:T(128)S(1)}, u32[]{:S(2)}) copy-start(s32[8]{0:T(128)S(1)} %get-tuple-element.40) | copy-start | bytes 100
  73.2 9.0 %copy-start.12 = (bf16[8,16,512]{2,1,0:T(8,128)(2,1)S(1)}, bf16[8,16,512]{2,1,0:T(8,128)(2,1)}, u32[]{:S(2)}) copy-start(bf16[8,16,512]{2,1,0:T(8,128)(2,1)} %param.86) | copy-start | bytes 393220
  99.4 9.0 %copy-start.68 = (s32[8]{0:T(128)S(1)}, s32[8]{0:T(128)}, u32[]{:S(2)}) copy-start(s32[8]{0:T(128)} %constant.634) | copy-start | bytes 100
  99.4 9.0 %copy-start.69 = (s32[64]{0:T(128)S(1)}, s32[64]{0:T(128)}, u32[]{:S(2)}) copy-start(s32[64]{0:T(128)} %constant.635) | copy-start | bytes 772
  107.6 7.7 %copy-start.6 = (bf16[8,64,512]{2,1,0:T(8,128)(2,1)S(1)}, bf16[8,64,512]{2,1,0:T(8,128)(2,1)}, u32[]{:S(2)}) copy-start(bf16[8,64,512]{2,1,0:T(8,128)(2,1)} %gather_fusion.71) | copy-start | bytes 1572868
  122.9 8.4 %copy-start.4 = (bf16[8,64,512]{2,1,0:T(8,128)(2,1)S(1)}, bf16[8,64,512]{2,1,0:T(8,128)(2,1)}, u32[]{:S(2)}) copy-start(bf16[8,64,512]{2,1,0:T(8,128)(2,1)} %gather_fusion.27) | copy-start | bytes 1572868
  122.9 8.4 %copy-start.5 = (bf16[8,64,512]{2,1,0:T(8,128)(2,1)S(1)}, bf16[8,64,512]{2,1,0:T(8,128)(2,1)}, u32[]{:S(2)}) copy-start(bf16[8,64,512]{2,1,0:T(8,128)(2,1)} %gather_fusion.75) | copy-start | bytes 1572868
  136.3 12.0 %copy-start.2 = (bf16[8,64,512]{2,1,0:T(8,128)(2,1)S(1)}, bf16[8,64,512]{2,1,0:T(8,128)(2,1)}, u32[]{:S(2)}) copy-start(bf16[8,64,512]{2,1,0:T(8,128)(2,1)} %gather_fusion.31) | copy-start | bytes 1572868
  136.3 12.0 %copy-start.3 = (bf16[8,64,512]{2,1,0:T(8,128)(2,1)S(1)}, bf16[8,64,512]{2,1,0:T(8,128)(2,1)}, u32[]{:S(2)}) copy-start(bf16[8,64,512]{2,1,0:T(8,128)(2,1)} %gather_fusion.79) | copy-start | bytes 1572868
  148.5 7.3 %copy-start.54 = (s32[8]{0:T(128)S(1)}, s32[8]{0:T(128)}, u32[]{:S(2)}) copy-start(s32[8]{0:T(128)} %get-tuple-element.135) | copy-start | bytes 100
  148.5 7.3 %copy-start.53 = (s32[8]{0:T(128)S(1)}, s32[8]{0:T(128)}, u32[]{:S(2)}) copy-start(s32[8]{0:T(128)} %get-tuple-element.134) | copy-start | bytes 100
  148.5 7.4 %copy-start.56 = (s32[8]{0:T(128)S(1)}, s32[8]{0:T(128)}, u32[]{:S(2)}) copy-start(s32[8]{0:T(128)} %get-tuple-element.133) | copy-start | bytes 100
  148.5 7.4 %copy-start.55 = (s32[8]{0:T(128)S(1)}, s32[8]{0:T(128)}, u32[]{:S(2)}) copy-start(s32[8]{0:T(128)} %get-tuple-element.132) | copy-start | bytes 100
  148.6 7.4 %copy-start.28 = (s32[896]{0:T(1024)S(1)}, s32[896]{0:T(1024)}, u32[]{:S(2)}) copy-start(s32[896]{0:T(1024)} %constant.605) | copy-start | bytes 10756
  148.6 7.4 %copy-start.29 = (s32[1000]{0:T(1024)S(1)}, s32[1000]{0:T(1024)}, u32[]{:S(2)}) copy-start(s32[1000]{0:T(1024)} %constant.640) | copy-start | bytes 12004
  148.6 11.4 %copy-start.30 = (bf16[896]{0:T(1024)(128)(2,1)S(1)}, bf16[896]{0:T(1024)(128)(2,1)}, u32[]{:S(2)}) copy-start(bf16[896]{0:T(1024)(128)(2,1)} %constant.267) | copy-start | bytes 5380
  160.0 7.6 %copy-start.25 = (bf16[27,16,64]{2,1,0:T(8,128)(2,1)S(1)}, bf16[27,16,64]{2,1,0:T(8,128)(2,1)}, u32[]{:S(2)}) copy-start(bf16[27,16,64]{2,1,0:T(8,128)(2,1)} %param.85) | copy-start | bytes 165892
  208.4 14.8 %copy-start.48 = (pred[8]{0:T(512)(128)(4,1)S(1)}, pred[8]{0:T(512)(128)(4,1)}, u32[]{:S(2)}) copy-start(pred[8]{0:T(512)(128)(4,1)} %get-tuple-element.184) | copy-start | bytes 28
  211.9 13.1 %copy-start.46 = (pred[8]{0:T(512)(128)(4,1)S(1)}, pred[8]{0:T(512)(128)(4,1)}, u32[]{:S(2)}) copy-start(pred[8]{0:T(512)(128)(4,1)} %get-tuple-element.185) | copy-start | bytes 28
  214.5 13.0 %copy-start.47 = (pred[8]{0:T(512)(128)(4,1)S(1)}, pred[8]{0:T(512)(128)(4,1)}, u32[]{:S(2)}) copy-start(pred[8]{0:T(512)(128)(4,1)} %get-tuple-element.183) | copy-start | bytes 28
  215.9 13.5 %copy-start.45 = (pred[8]{0:T(512)(128)(4,1)S(1)}, pred[8]{0:T(512)(128)(4,1)}, u32[]{:S(2)}) copy-start(pred[8]{0:T(512)(128)(4,1)} %get-tuple-element.182) | copy-start | bytes 28
  225.0 19.0 %copy-start.44 = (pred[8]{0:T(512)(128)(4,1)S(1)}, pred[8]{0:T(512)(128)(4,1)}, u32[]{:S(2)}) copy-start(pred[8]{0:T(512)(128)(4,1)} %get-tuple-element.181) | copy-start | bytes 28
  229.4 24.0 %copy-start.20 = (bf16[8,64,64]{2,1,0:T(8,128)(2,1)S(1)}, bf16[8,64,64]{2,1,0:T(8,128)(2,1)}, u32[]{:S(2)}) copy-start(bf16[8,64,64]{2,1,0:T(8,128)(2,1)} %gather_fusion.9) | copy-start | bytes 196612
  229.4 24.0 %copy-start.43 = (pred[8]{0:T(512)(128)(4,1)S(1)}, pred[8]{0:T(512)(128)(4,1)}, u32[]{:S(2)}) copy-start(pred[8]{0:T(512)(128)(4,1)} %get-tuple-element.180) | copy-start | bytes 28
  242.4 21.4 %copy-start.19 = (bf16[8,64,64]{2,1,0:T(8,128)(2,1)S(1)}, bf16[8,64,64]{2,1,0:T(8,128)(2,1)}, u32[]{:S(2)}) copy-start(bf16[8,64,64]{2,1,0:T(8,128)(2,1)} %gather_fusion.60) | copy-start | bytes 196612
  242.4 21.4 %copy-start.35 = (pred[8]{0:T(512)(128)(4,1)S(1)}, pred[8]{0:T(512)(128)(4,1)}, u32[]{:S(2)}) copy-start(pred[8]{0:T(512)(128)(4,1)} %get-tuple-element.177) | copy-start | bytes 28
  251.2 18.1 %copy-start.34 = (pred[8]{0:T(512)(128)(4,1)S(1)}, pred[8]{0:T(512)(128)(4,1)}, u32[]{:S(2)}) copy-start(pred[8]{0:T(512)(128)(4,1)} %get-tuple-element.176) | copy-start | bytes 28
  259.9 13.8 %copy-start.18 = (bf16[8,64,64]{2,1,0:T(8,128)(2,1)S(1)}, bf16[8,64,64]{2,1,0:T(8,128)(2,1)}, u32[]{:S(2)}) copy-start(bf16[8,64,64]{2,1,0:T(8,128)(2,1)} %gather_fusion.82) | copy-start | bytes 196612
  259.9 13.7 %copy-start.40 = (pred[8]{0:T(512)(128)(4,1)S(1)}, pred[8]{0:T(512)(128)(4,1)}, u32[]{:S(2)}) copy-start(pred[8]{0:T(512)(128)(4,1)} %get-tuple-element.165) | copy-start | bytes 28
  267.9 9.6 %copy-start.39 = (pred[8]{0:T(512)(128)(4,1)S(1)}, pred[8]{0:T(512)(128)(4,1)}, u32[]{:S(2)}) copy-start(pred[8]{0:T(512)(128)(4,1)} %get-tuple-element.163) | copy-start | bytes 28
  281.5 13.3 %copy-start.16 = (bf16[64,8,64]{2,1,0:T(8,128)(2,1)S(1)}, bf16[64,8,64]{2,1,0:T(8,128)(2,1)}, u32[]{:S(2)}) copy-start(bf16[64,8,64]{2,1,0:T(8,128)(2,1)} %gather_fusion.8) | copy-start | bytes 196612
  281.5 13.3 %copy-start.17 = (bf16[64,8,64]{2,1,0:T(8,128)(2,1)S(1)}, bf16[64,8,64]{2,1,0:T(8,128)(2,1)}, u32[]{:S(2)}) copy-start(bf16[64,8,64]{2,1,0:T(8,128)(2,1)} %gather_fusion.56) | copy-start | bytes 196612
  281.5 13.2 %copy-start.31 = (pred[64]{0:T(512)(128)(4,1)S(1)}, pred[64]{0:T(512)(128)(4,1)}, u32[]{:S(2)}) copy-start(pred[64]{0:T(512)(128)(4,1)} %broadcast_compare_fusion.2) | copy-start | bytes 196
  281.6 13.9 %copy-start.33 = (pred[8]{0:T(512)(128)(4,1)S(1)}, pred[8]{0:T(512)(128)(4,1)}, u32[]{:S(2)}) copy-start(pred[8]{0:T(512)(128)(4,1)} %get-tuple-element.179) | copy-start | bytes 28
  281.6 15.8 %copy-start.32 = (pred[8]{0:T(512)(128)(4,1)S(1)}, pred[8]{0:T(512)(128)(4,1)}, u32[]{:S(2)}) copy-start(pred[8]{0:T(512)(128)(4,1)} %broadcast_compare_fusion.1) | copy-start | bytes 28
  284.0 24.0 %copy-start.1 = (bf16[512,8,64]{2,1,0:T(8,128)(2,1)S(1)}, bf16[512,8,64]{2,1,0:T(8,128)(2,1)}, u32[]{:S(2)}) copy-start(bf16[512,8,64]{2,1,0:T(8,128)(2,1)} %gather_fusion.72) | copy-start | bytes 1572868
  284.0 24.0 %copy-start.57 = (pred[512]{0:T(512)(128)(4,1)S(1)}, pred[512]{0:T(512)(128)(4,1)}, u32[]{:S(2)}) copy-start(pred[512]{0:T(512)(128)(4,1)} %broadcast_compare_fusion) | copy-start | bytes 1540
  308.0 8.7 %copy-start.52 = (pred[8]{0:T(512)(128)(4,1)S(1)}, pred[8]{0:T(512)(128)(4,1)}, u32[]{:S(2)}) copy-start(pred[8]{0:T(512)(128)(4,1)} %get-tuple-element.164) | copy-start | bytes 28
  308.0 10.5 %copy-start.15 = (bf16[64,8,64]{2,1,0:T(8,128)(2,1)S(1)}, bf16[64,8,64]{2,1,0:T(8,128)(2,1)}, u32[]{:S(2)}) copy-start(bf16[64,8,64]{2,1,0:T(8,128)(2,1)} %gather_fusion.88) | copy-start | bytes 196612
  308.1 12.1 %copy-start.51 = (pred[8]{0:T(512)(128)(4,1)S(1)}, pred[8]{0:T(512)(128)(4,1)}, u32[]{:S(2)}) copy-start(pred[8]{0:T(512)(128)(4,1)} %get-tuple-element.160) | copy-start | bytes 28
  308.1 13.4 %copy-start.50 = (pred[8]{0:T(512)(128)(4,1)S(1)}, pred[8]{0:T(512)(128)(4,1)}, u32[]{:S(2)}) copy-start(pred[8]{0:T(512)(128)(4,1)} %get-tuple-element.158) | copy-start | bytes 28
  (29 other events, 127.4 us)
Sparse Core Ops, SparseCore 0:
  346.3 338.5 all-reduce.9
where the time goes:
time: 703 us; the launch traced here: 694 us
  waiting for transfers between devices  292 us (42%)
  local copies, waits for them, and re-layouts  236 us (34%)
  other arithmetic  54.3 us (8%)
  blocking collectives  43.1 us (6%)
  matrix products  40.2 us (6%)
  between operations  16.1 us (2%)
  starting transfers between devices  11.7 us (2%)
    psum x1, waiting for transfers between devices, body(): summed = lax.psum(jnp.stack(kernel_terms), 'space')  292 us
    gather x54, local copies, waits for them, and re-layouts, assemble(): picked = jnp.take(sources[step_x], local_ids, axis=0)  60.5 us
    gather x38, local copies, waits for them, and re-layouts, assemble(): pieces.append(jnp.take(picked, jnp.asarray(lists[index_k]), axis=2))  54.5 us
    select_n x38, local copies, waits for them, and re-layouts, assemble(): picked = jnp.take(sources[step_x], local_ids, axis=0)  42.1 us
    unnamed x183, local copies, waits for them, and re-layouts  30.2 us
    all_gather x2, blocking collectives, spread(): entire = lax.all_gather(own_part, 'chan', axis=2, tiled=True)  28.9 us
    select_n x38, other arithmetic, assemble(): picked = jnp.take(sources[step_x], local_ids, axis=0)  23.9 us
    gather x4, local copies, waits for them, and re-layouts, assemble(): flat = jnp.take(joined, jnp.asarray(order), axis=2)  19.1 us
  transfers between devices with their start and end apart: 5, of which 1 were waited for; matrix products, arithmetic and copies ran while one was open for 27% of the time, Pallas kernels for 0%

commit v1 on v0

--- a/solution.py
+++ b/solution.py
@@ -69,7 +69,9 @@
 
 
 def spread(own_part):
-    entire = lax.all_gather(own_part, "chan", axis=2, tiled=True)
+    placed = jnp.stack([own_part for _ in range(jax.lax.axis_size("chan"))])
+    b_next = jax.lax.all_to_all(placed, "chan", 0, 0)
+    entire = jnp.concatenate(b_next, axis=2)
     before_plane, after_plane = neighbour_planes(entire)
     return (entire, before_plane, after_plane)
 

time: 703 us -> 775 us (1.10)
  local copies, waits for them, and re-layouts: 236 us -> 294 us
  blocking collectives: 43.1 us -> 14.2 us
  other arithmetic: 54.3 us -> 82.4 us
  starting transfers between devices: 11.7 us -> 21.6 us
    all_gather x2 -> x0, blocking collectives: 28.9 us -> none  [spread(): entire = lax.all_gather(own_part, 'chan', axis=2, tiled=True)]
    select_n x38, local copies, waits for them, and re-layouts: 42.1 us -> 66.8 us  [assemble(): picked = jnp.take(sources[step_x], local_ids, axis=0)]
    gather x38, local copies, waits for them, and re-layouts: 54.5 us -> 70 us  [assemble(): pieces.append(jnp.take(picked, jnp.asarray(lists[index_k]), axis=2))]
    gather x36, other arithmetic: 2.57 us -> 16.2 us
    select_n x38, other arithmetic: 23.9 us -> 34.4 us  [assemble(): picked = jnp.take(sources[step_x], local_ids, axis=0)]
    all_to_all x0 -> x2, starting transfers between devices: none -> 8.56 us  [spread(): b_next = jax.lax.all_to_all(placed, 'chan', 0, 0)]
    unnamed x183 -> x197, local copies, waits for them, and re-layouts: 30.2 us -> 34.4 us
  transfers between devices with their start and end apart: 5 -> 7, of which waited for: 1 -> 2; matrix products, arithmetic and copies ran while one was open for 27% -> 27% of each run, Pallas kernels for 0% -> 0%
where the time goes in v1:
time: 775 us; the launch traced here: 766 us
  waiting for transfers between devices  298 us (38%)
  local copies, waits for them, and re-layouts  294 us (38%)
  other arithmetic  82.4 us (11%)
  matrix products  40.2 us (5%)
  starting transfers between devices  21.6 us (3%)
  between operations  15.4 us (2%)
  blocking collectives  14.2 us (2%)
    psum x1, waiting for transfers between devices, body(): summed = lax.psum(jnp.stack(kernel_terms), 'space')  291 us
    gather x38, local copies, waits for them, and re-layouts, assemble(): pieces.append(jnp.take(picked, jnp.asarray(lists[index_k]), axis=2))  70 us
    gather x54, local copies, waits for them, and re-layouts, assemble(): picked = jnp.take(sources[step_x], local_ids, axis=0)  68.1 us
    select_n x38, local copies, waits for them, and re-layouts, assemble(): picked = jnp.take(sources[step_x], local_ids, axis=0)  66.8 us
    select_n x38, other arithmetic, assemble(): picked = jnp.take(sources[step_x], local_ids, axis=0)  34.4 us
    unnamed x197, local copies, waits for them, and re-layouts  34.4 us
    gather x4, local copies, waits for them, and re-layouts, assemble(): flat = jnp.take(joined, jnp.asarray(order), axis=2)  19 us
    select_n x14, local copies, waits for them, and re-layouts, assemble(): pieces.append(jnp.take(picked, jnp.asarray(lists[index_k]), axis=2))  16.5 us
  transfers between devices with their start and end apart: 7, of which 2 were waited for; matrix products, arithmetic and copies ran while one was open for 27% of the time, Pallas kernels for 0%

profile of v1, /device:TPU:2, one launch (start us, length us, event | category | flops | bytes accessed | tf_op | source)
XLA Modules:
  0.0 766.0 jit_solution(17260468396241331615)
XLA Ops:
  9.0 4.5 all-to-all-start
  39.9 3.6 gather_fusion
  43.5 4.5 multiply_bitcast_fusion
  49.8 14.2 %all_gather.3 = bf16[27,64,64]{2,1,0:T(8,128)(2,1)} all-gather(bf16[27,16,64]{2,1,0:T(8,128)(2,1)S(1)} %copy-done.32), channel_id=1, replica_groups=mesh['space'=128,'chan'=4] {'chan'}, dimensions={1}, use_global_device_ids=true | all-gather | bytes 276480 | tf_op jit(solution)/shard_map/all_gather | solution.py:138
  68.5 4.1 all-to-all-start.1
  73.9 6.8 all-to-all-done.1
  102.1 2.0 collective-permute-start
  104.2 3.6 collective-permute-start.1
  107.8 1.9 collective-permute-start.2
  109.7 5.4 collective-permute-start.3
  115.2 2.4 broadcast_select_fusion.16
  128.5 2.3 broadcast_select_fusion
  132.5 2.8 copy.199
  135.3 2.7 copy.200
  138.1 2.8 copy.201
  142.6 1.9 gather_fusion.16
  144.5 1.9 gather_fusion.64
  148.1 2.6 gather_fusion.18
  150.8 2.6 gather_fusion.66
  155.1 2.0 gather_fusion.20
  157.1 1.9 gather_fusion.68
  160.7 2.6 gather_fusion.22
  163.3 2.6 gather_fusion.70
  167.5 2.0 gather_fusion.24
  171.3 2.8 copy.203
  174.1 2.8 copy.233
  176.9 2.7 gather_fusion.26
  179.6 2.6 gather_fusion.74
  183.9 2.8 copy.205
  188.4 2.0 gather_fusion.28
  190.4 1.9 gather_fusion.76
  194.0 2.6 gather_fusion.30
  196.6 2.6 gather_fusion.78
  199.2 2.8 copy.206
  203.6 1.9 gather_fusion.32
  205.6 1.9 gather_fusion.80
  282.0 2.2 gather_fusion.8
  284.2 2.2 gather_fusion.56
  294.4 1.8 slice_select_fusion.1
  343.7 2.2 gather_fusion.88
  381.4 3.1 bitcast_dynamic-update-slice_fusion
  395.8 5.1 gather_fusion.47
  400.9 2.0 copy.220
  419.7 9.2 %gather_fusion.95 = bf16[1000,8,64]{2,1,0:T(8,128)(2,1)} fusion(bf16[8,64,1000]{1,0,2:T(8,128)(2,1)} %get-tuple-element.60, s32[1024]{0:T(1024)S(1)} %get-tuple-element.187), kind=kCustom, calls=%fused_computation.94.clone | custom fusion | bytes 2052000 | tf_op jit(solution)/shard_map/jit(_take)/gather | solution.py:98
  428.9 2.7 copy.250
  456.1 1.9 copy.252
  461.2 1.9 copy.221
  466.3 291.1 %all-reduce.10.cloned.1.call-done = f32[27,16,64]{2,1,0:T(8,128)} async-done(((f32[27,16,64]{2,1,0:T(8,128)}), f32[27,16,64]{2,1,0:T(8,128)}) %all-reduce.10.cloned.1.call-update) | async-done | bytes 110608 | tf_op jit(solution)/shard_map/psum | solution.py:136
  (530 shorter events, 312.0 us)
Async XLA Ops:
  7.2 32.7 %copy-start.36 = (s32[896]{0:T(1024)S(1)}, s32[896]{0:T(1024)}, u32[]{:S(2)}) copy-start(s32[896]{0:T(1024)} %constant.605) | copy-start | bytes 10756
  7.2 32.7 %copy-start.37 = (s32[1000]{0:T(1024)S(1)}, s32[1000]{0:T(1024)}, u32[]{:S(2)}) copy-start(s32[1000]{0:T(1024)} %constant.640) | copy-start | bytes 12004
  7.2 36.3 %copy-start.38 = (bf16[896]{0:T(1024)(128)(2,1)S(1)}, bf16[896]{0:T(1024)(128)(2,1)}, u32[]{:S(2)}) copy-start(bf16[896]{0:T(1024)(128)(2,1)} %constant.267) | copy-start | bytes 5380
  7.2 31.8 %copy-start.23 = (bf16[8,16,512]{2,1,0:T(8,128)(2,1)S(1)}, bf16[8,16,512]{2,1,0:T(8,128)(2,1)}, u32[]{:S(2)}) copy-start(bf16[8,16,512]{2,1,0:T(8,128)(2,1)} %param.86) | copy-start | bytes 393220
  9.0 58.6 %all-to-all-start = ((bf16[4,1,8,16,512]{4,3,2,1,0:T(8,128)(2,1)}), bf16[4,1,8,16,512]{4,3,2,1,0:T(8,128)(2,1)S(1)}, u32[]{:S(2)}, u32[]{:S(2)}) async-start(bf16[4,1,8,16,512]{4,3,2,1,0:T(8,128)(2,1)} %stack.90), calls=%async_computation | async-start | bytes 1048576 | tf_op jit(solution)/shard_map/all_to_all | solution.py:73
  28.9 55.4 %copy-start.35 = (s32[1024]{0:T(1024)}, s32[1024]{0:T(1024)S(1)}, u32[]{:S(2)}) copy-start(s32[1024]{0:T(1024)S(1)} %pad_clamp_fusion.27) | copy-start | bytes 12292
  48.0 16.1 %copy-start.62 = (s32[512]{0:T(512)S(1)}, s32[512]{0:T(512)}, u32[]{:S(2)}) copy-start(s32[512]{0:T(512)} %constant.641) | copy-start | bytes 6148
  48.0 16.1 %copy-start.78 = (s32[8]{0:T(128)S(1)}, s32[8]{0:T(128)}, u32[]{:S(2)}) copy-start(s32[8]{0:T(128)} %constant.631) | copy-start | bytes 100
  48.0 16.1 %copy-start.76 = (s32[8]{0:T(128)S(1)}, s32[8]{0:T(128)}, u32[]{:S(2)}) copy-start(s32[8]{0:T(128)} %constant.632) | copy-start | bytes 100
  48.0 16.1 %copy-start.77 = (s32[64]{0:T(128)S(1)}, s32[64]{0:T(128)}, u32[]{:S(2)}) copy-start(s32[64]{0:T(128)} %constant.633) | copy-start | bytes 772
  48.0 16.7 %copy-start.74 = (s32[8]{0:T(128)S(1)}, s32[8]{0:T(128)}, u32[]{:S(2)}) copy-start(s32[8]{0:T(128)} %constant.634) | copy-start | bytes 100
  48.0 16.7 %copy-start.75 = (s32[64]{0:T(128)S(1)}, s32[64]{0:T(128)}, u32[]{:S(2)}) copy-start(s32[64]{0:T(128)} %constant.635) | copy-start | bytes 772
  48.0 17.9 %copy-start.72 = (s32[8]{0:T(128)S(1)}, s32[8]{0:T(128)}, u32[]{:S(2)}) copy-start(s32[8]{0:T(128)} %constant.636) | copy-start | bytes 100
  48.0 17.9 %copy-start.73 = (s32[64]{0:T(128)S(1)}, s32[64]{0:T(128)}, u32[]{:S(2)}) copy-start(s32[64]{0:T(128)} %constant.637) | copy-start | bytes 772
  68.5 12.2 %all-to-all-start.1 = ((bf16[4,1,8,16,512]{4,3,2,1,0:T(8,128)(2,1)}), bf16[4,1,8,16,512]{4,3,2,1,0:T(8,128)(2,1)S(1)}, u32[]{:S(2)}, u32[]{:S(2)}) async-start(bf16[4,1,8,16,512]{4,3,2,1,0:T(8,128)(2,1)} %stack.91), calls=%async_computation.1 | async-start | bytes 1048576 | tf_op jit(solution)/shard_map/all_to_all | solution.py:73
  72.6 684.7 %all-reduce.10.cloned.1.call-start = ((), (), s32[]{:S(2)}) async-start(), calls=%async_computation.2 | async-start | bytes 442368 | tf_op jit(solution)/shard_map/psum | solution.py:136
  102.1 15.5 %copy-start.61 = (pred[8]{0:T(512)(128)(4,1)S(1)}, pred[8]{0:T(512)(128)(4,1)}, u32[]{:S(2)}) copy-start(pred[8]{0:T(512)(128)(4,1)} %get-tuple-element.175) | copy-start | bytes 28
  102.1 106.4 %collective-permute-start = (bf16[1,8,64,512]{3,2,1,0:T(8,128)(2,1)}, bf16[1,8,64,512]{3,2,1,0:T(8,128)(2,1)}, u32[]{:S(2)}, u32[]{:S(2)}) collective-permute-start(bf16[1,8,64,512]{3,2,1,0:T(8,128)(2,1)} %bitcast.677), channel_id=1, source_target_pairs={{0,4},{4,8},{8,12},{12,16},{16,20},{20,24},{24,28},{28,32},{32,36}... | collective-permute-start | bytes 1572872 | tf_op jit(solution)/shard_map/ppermute | solution.py:14
  104.2 128.6 %collective-permute-start.1 = (bf16[1,8,64,512]{3,2,1,0:T(8,128)(2,1)}, bf16[1,8,64,512]{3,2,1,0:T(8,128)(2,1)}, u32[]{:S(2)}, u32[]{:S(2)}) collective-permute-start(bf16[1,8,64,512]{3,2,1,0:T(8,128)(2,1)} %bitcast.678), channel_id=1, source_target_pairs={{4,0},{8,4},{12,8},{16,12},{20,16},{24,20},{28,24},{32,28},{36,32}... | collective-permute-start | bytes 1572872 | tf_op jit(solution)/shard_map/ppermute | solution.py:14
  107.8 99.7 %collective-permute-start.2 = (bf16[1,8,64,512]{3,2,1,0:T(8,128)(2,1)}, bf16[1,8,64,512]{3,2,1,0:T(8,128)(2,1)}, u32[]{:S(2)}, u32[]{:S(2)}) collective-permute-start(bf16[1,8,64,512]{3,2,1,0:T(8,128)(2,1)} %bitcast.680), channel_id=1, source_target_pairs={{0,4},{4,8},{8,12},{12,16},{16,20},{20,24},{24,28},{28,32},{32,36}... | collective-permute-start | bytes 1572872 | tf_op jit(solution)/shard_map/ppermute | solution.py:14
  109.7 123.9 %collective-permute-start.3 = (bf16[1,8,64,512]{3,2,1,0:T(8,128)(2,1)}, bf16[1,8,64,512]{3,2,1,0:T(8,128)(2,1)}, u32[]{:S(2)}, u32[]{:S(2)}) collective-permute-start(bf16[1,8,64,512]{3,2,1,0:T(8,128)(2,1)} %bitcast.681), channel_id=1, source_target_pairs={{4,0},{8,4},{12,8},{16,12},{20,16},{24,20},{28,24},{32,28},{36,32}... | collective-permute-start | bytes 1572872 | tf_op jit(solution)/shard_map/ppermute | solution.py:14
  155.1 11.6 %copy-start.4 = (bf16[8,64,512]{2,1,0:T(8,128)(2,1)S(1)}, bf16[8,64,512]{2,1,0:T(8,128)(2,1)}, u32[]{:S(2)}) copy-start(bf16[8,64,512]{2,1,0:T(8,128)(2,1)} %get-tuple-element.98) | copy-start | bytes 1572868
  171.3 10.9 %copy-start.3 = (bf16[8,64,512]{2,1,0:T(8,128)(2,1)S(1)}, bf16[8,64,512]{2,1,0:T(8,128)(2,1)}, u32[]{:S(2)}) copy-start(bf16[8,64,512]{2,1,0:T(8,128)(2,1)} %get-tuple-element.91) | copy-start | bytes 1572868
  188.4 13.6 %copy-start.1 = (bf16[8,64,512]{2,1,0:T(8,128)(2,1)S(1)}, bf16[8,64,512]{2,1,0:T(8,128)(2,1)}, u32[]{:S(2)}) copy-start(bf16[8,64,512]{2,1,0:T(8,128)(2,1)} %get-tuple-element.86) | copy-start | bytes 1572868
  237.3 18.7 %copy-start.51 = (pred[8]{0:T(512)(128)(4,1)S(1)}, pred[8]{0:T(512)(128)(4,1)}, u32[]{:S(2)}) copy-start(pred[8]{0:T(512)(128)(4,1)} %get-tuple-element.185) | copy-start | bytes 28
  241.5 16.4 %copy-start.70 = (pred[8]{0:T(512)(128)(4,1)S(1)}, pred[8]{0:T(512)(128)(4,1)}, u32[]{:S(2)}) copy-start(pred[8]{0:T(512)(128)(4,1)} %compare_and_fusion.29) | copy-start | bytes 28
  245.6 14.8 %copy-start.50 = (pred[8]{0:T(512)(128)(4,1)S(1)}, pred[8]{0:T(512)(128)(4,1)}, u32[]{:S(2)}) copy-start(pred[8]{0:T(512)(128)(4,1)} %get-tuple-element.184) | copy-start | bytes 28
  247.8 14.6 %copy-start.49 = (pred[8]{0:T(512)(128)(4,1)S(1)}, pred[8]{0:T(512)(128)(4,1)}, u32[]{:S(2)}) copy-start(pred[8]{0:T(512)(128)(4,1)} %get-tuple-element.183) | copy-start | bytes 28
  257.9 18.9 %copy-start.47 = (pred[8]{0:T(512)(128)(4,1)S(1)}, pred[8]{0:T(512)(128)(4,1)}, u32[]{:S(2)}) copy-start(pred[8]{0:T(512)(128)(4,1)} %get-tuple-element.182) | copy-start | bytes 28
  262.3 24.0 %copy-start.29 = (bf16[8,64,64]{2,1,0:T(8,128)(2,1)S(1)}, bf16[8,64,64]{2,1,0:T(8,128)(2,1)}, u32[]{:S(2)}) copy-start(bf16[8,64,64]{2,1,0:T(8,128)(2,1)} %gather_fusion.9) | copy-start | bytes 196612
  262.3 24.0 %copy-start.68 = (pred[8]{0:T(512)(128)(4,1)S(1)}, pred[8]{0:T(512)(128)(4,1)}, u32[]{:S(2)}) copy-start(pred[8]{0:T(512)(128)(4,1)} %get-tuple-element.181) | copy-start | bytes 28
  270.6 23.8 %copy-start.45 = (pred[8]{0:T(512)(128)(4,1)S(1)}, pred[8]{0:T(512)(128)(4,1)}, u32[]{:S(2)}) copy-start(pred[8]{0:T(512)(128)(4,1)} %get-tuple-element.179) | copy-start | bytes 28
  275.3 22.9 %copy-start.43 = (pred[8]{0:T(512)(128)(4,1)S(1)}, pred[8]{0:T(512)(128)(4,1)}, u32[]{:S(2)}) copy-start(pred[8]{0:T(512)(128)(4,1)} %get-tuple-element.178) | copy-start | bytes 28
  284.2 22.2 %copy-start.42 = (pred[8]{0:T(512)(128)(4,1)S(1)}, pred[8]{0:T(512)(128)(4,1)}, u32[]{:S(2)}) copy-start(pred[8]{0:T(512)(128)(4,1)} %get-tuple-element.177) | copy-start | bytes 28
  294.4 21.2 %copy-start.48 = (pred[8]{0:T(512)(128)(4,1)S(1)}, pred[8]{0:T(512)(128)(4,1)}, u32[]{:S(2)}) copy-start(pred[8]{0:T(512)(128)(4,1)} %get-tuple-element.165) | copy-start | bytes 28
  304.9 24.2 %copy-start.46 = (pred[8]{0:T(512)(128)(4,1)S(1)}, pred[8]{0:T(512)(128)(4,1)}, u32[]{:S(2)}) copy-start(pred[8]{0:T(512)(128)(4,1)} %get-tuple-element.163) | copy-start | bytes 28
  314.6 22.6 %copy-start.44 = (pred[8]{0:T(512)(128)(4,1)S(1)}, pred[8]{0:T(512)(128)(4,1)}, u32[]{:S(2)}) copy-start(pred[8]{0:T(512)(128)(4,1)} %get-tuple-element.162) | copy-start | bytes 28
  322.2 23.7 %copy-start.53 = (pred[8]{0:T(512)(128)(4,1)S(1)}, pred[8]{0:T(512)(128)(4,1)}, u32[]{:S(2)}) copy-start(pred[8]{0:T(512)(128)(4,1)} %get-tuple-element.161) | copy-start | bytes 28
  335.6 22.8 %copy-start.52 = (pred[8]{0:T(512)(128)(4,1)S(1)}, pred[8]{0:T(512)(128)(4,1)}, u32[]{:S(2)}) copy-start(pred[8]{0:T(512)(128)(4,1)} %get-tuple-element.159) | copy-start | bytes 28
  346.7 21.4 %copy-start.27 = (bf16[64,8,64]{2,1,0:T(8,128)(2,1)S(1)}, bf16[64,8,64]{2,1,0:T(8,128)(2,1)}, u32[]{:S(2)}) copy-start(bf16[64,8,64]{2,1,0:T(8,128)(2,1)} %gather_fusion.8) | copy-start | bytes 196612
  346.7 21.4 %copy-start.28 = (bf16[64,8,64]{2,1,0:T(8,128)(2,1)S(1)}, bf16[64,8,64]{2,1,0:T(8,128)(2,1)}, u32[]{:S(2)}) copy-start(bf16[64,8,64]{2,1,0:T(8,128)(2,1)} %gather_fusion.56) | copy-start | bytes 196612
  346.7 21.4 %copy-start.41 = (pred[64]{0:T(512)(128)(4,1)S(1)}, pred[64]{0:T(512)(128)(4,1)}, u32[]{:S(2)}) copy-start(pred[64]{0:T(512)(128)(4,1)} %broadcast_compare_fusion.2) | copy-start | bytes 196
  348.4 20.5 %copy-start.40 = (pred[8]{0:T(512)(128)(4,1)S(1)}, pred[8]{0:T(512)(128)(4,1)}, u32[]{:S(2)}) copy-start(pred[8]{0:T(512)(128)(4,1)} %get-tuple-element.180) | copy-start | bytes 28
  348.4 22.4 %copy-start.39 = (pred[8]{0:T(512)(128)(4,1)S(1)}, pred[8]{0:T(512)(128)(4,1)}, u32[]{:S(2)}) copy-start(pred[8]{0:T(512)(128)(4,1)} %broadcast_compare_fusion.1) | copy-start | bytes 28
  357.4 23.9 %copy-start.66 = (pred[512]{0:T(512)(128)(4,1)S(1)}, pred[512]{0:T(512)(128)(4,1)}, u32[]{:S(2)}) copy-start(pred[512]{0:T(512)(128)(4,1)} %broadcast_compare_fusion) | copy-start | bytes 1540
  381.3 10.9 %copy-start.26 = (bf16[64,8,64]{2,1,0:T(8,128)(2,1)S(1)}, bf16[64,8,64]{2,1,0:T(8,128)(2,1)}, u32[]{:S(2)}) copy-start(bf16[64,8,64]{2,1,0:T(8,128)(2,1)} %gather_fusion.88) | copy-start | bytes 196612
  381.4 12.5 %copy-start.64 = (pred[8]{0:T(512)(128)(4,1)S(1)}, pred[8]{0:T(512)(128)(4,1)}, u32[]{:S(2)}) copy-start(pred[8]{0:T(512)(128)(4,1)} %get-tuple-element.160) | copy-start | bytes 28
  381.4 13.8 %copy-start.65 = (pred[8]{0:T(512)(128)(4,1)S(1)}, pred[8]{0:T(512)(128)(4,1)}, u32[]{:S(2)}) copy-start(pred[8]{0:T(512)(128)(4,1)} %get-tuple-element.158) | copy-start | bytes 28
  (38 other events, 145.0 us)
Sparse Core Ops, SparseCore 0:
  419.8 337.4 all-reduce.9
